TPU v7x, 32 devices: a whole 2x2x4 slice. The times are simulated.
32 devices in a mesh: grp: 8 (over y, x, core), loc: 4 (over z).
Axes of the slice: x: 2, y: 2, z: 4, core: 2. Of those that a mesh axis runs over, the one named last changes fastest.
Arguments:
- tokens: bfloat16 [4096, 7168], P(('grp', 'loc')), may hold values from -6 to 6
- route: int32 [4096, 1], P(('grp', 'loc')), may hold values from 0 to 7; in each aligned block of 128 rows (0 to 127, 128 to 255, ...) at most 20 rows name the same one
- gate_prob: float32 [4096, 1], P(('grp', 'loc')), may hold values from 0.25 to 1
- w_gate: bfloat16 [32, 7168, 256], P(('grp', 'loc')), may hold values from -0.0625 to 0.0625
- w_up: bfloat16 [32, 7168, 256], P(('grp', 'loc')), may hold values from -0.0625 to 0.0625
- w_down: bfloat16 [32, 256, 7168], P(('grp', 'loc')), may hold values from -0.1875 to 0.1875
- partner: int32 [32, 2], replicated, may hold values from 0 to 31, as said below
Outputs:
- mixed: bfloat16 [4096, 7168], P(('grp', 'loc'))
Inputs may be any that keep to these rules, and one draw needn't show every extreme that they name: `route`: within the 128 rows of one device no expert is named more than 20 times, a bound that some block reaches. partner[i, h] is slot i itself, slot i - 1 or slot i + 1, cyclically over all slots.
All inputs are finite; a program needn't handle non-finite values.
Results may differ from a plain program's by a relative error of at most 0.0056.
Values may be sent and summed in bfloat16 or wider, within the bound.
A program may use at most 192 MiB of HBM per device.

v0:
```python
import jax
import jax.numpy as jnp
from jax import lax
from jax.sharding import PartitionSpec as P

SPAN = 4


def shifted(block, axis, distance):
    devices = range(lax.axis_size(axis))
    route = [((i - distance) % len(devices), i) for i in devices]
    return lax.ppermute(block, axis, route)


def expert_pass(row_block, gate_block, up_block, down_block):
    gate_part = jnp.dot(row_block, gate_block, preferred_element_type=jnp.float32)
    up_part = jnp.dot(row_block, up_block, preferred_element_type=jnp.float32)
    hidden = (jax.nn.silu(gate_part) * up_part).astype(jnp.bfloat16)
    return jnp.dot(hidden, down_block, preferred_element_type=jnp.float32).astype(jnp.bfloat16)


def migrate(w_gate, w_up, w_down, partner, own_index, slots_all):
    lower = shifted((w_gate, w_up, w_down), ("grp", "loc"), 1)
    upper = shifted((w_gate, w_up, w_down), ("grp", "loc"), -1)
    own_blocks = (w_gate, w_up, w_down)
    mine = partner[own_index]
    chosen = []
    for which in range(2):
        offset = (mine[which] - own_index) % slots_all
        chosen.append(
            tuple(
                (
                    jnp.where(
                        offset == slots_all - 1,
                        low_part,
                        jnp.where(offset == 1, up_piece, own_part),
                    )
                    for low_part, up_piece, own_part in zip(lower, upper, own_blocks)
                )
            )
        )
    half = w_gate.shape[2] // 2
    gate_block = jnp.concatenate([chosen[0][0][0][:, :half], chosen[1][0][0][:, half:]], axis=1)
    up_block = jnp.concatenate([chosen[0][1][0][:, :half], chosen[1][1][0][:, half:]], axis=1)
    down_block = jnp.concatenate([chosen[0][2][0][:half], chosen[1][2][0][half:]], axis=0)
    return (gate_block, up_block, down_block)


def make_picker(owner_expert, flat_route, slot_rank, capacity):
    matches = owner_expert[:, None] == flat_route[None, :]
    slot_match = jnp.arange(capacity, dtype=jnp.int32)[:, None] == slot_rank[None, :]
    return (matches[:, None, :] & slot_match[None, :, :]).reshape(
        owner_expert.shape[0] * capacity, -1
    )


def body(tokens, route, gate_prob, w_gate, w_up, w_down, partner):
    slots_all = lax.axis_size(("grp", "loc"))
    own_index = lax.axis_index(("grp", "loc"))
    tok_count, top_count = route.shape
    width = tokens.shape[1]
    capacity = max(2, tok_count * top_count * SPAN * 5 // (4 * slots_all))
    experts_all = slots_all // SPAN
    flat_route = route.reshape(-1)
    flat_gate = gate_prob.reshape(-1)
    onehot = (flat_route[:, None] == jnp.arange(experts_all, dtype=jnp.int32)[None, :]).astype(
        jnp.int32
    )
    slot_rank = jnp.sum(jnp.cumsum(onehot, axis=0) * onehot, axis=1) - 1
    assigned = jnp.repeat(tokens, top_count, axis=0)
    gate_block, up_block, down_block = migrate(w_gate, w_up, w_down, partner, own_index, slots_all)
    block_expert = jnp.arange(slots_all, dtype=jnp.int32) // SPAN
    picker = make_picker(block_expert, flat_route, slot_rank, capacity).astype(jnp.bfloat16)
    outgoing = jnp.dot(picker, assigned, preferred_element_type=jnp.float32).astype(jnp.bfloat16)
    outgoing = outgoing.reshape(slots_all, capacity, width)
    received = lax.all_to_all(outgoing, ("grp", "loc"), split_axis=0, concat_axis=0, tiled=True)
    result = expert_pass(received.reshape(-1, width), gate_block, up_block, down_block)
    returned = lax.all_to_all(
        result.reshape(received.shape), ("grp", "loc"), split_axis=0, concat_axis=0, tiled=True
    )
    returned = returned.reshape(slots_all * capacity, width)
    expert_out = lax.dot_general(
        picker, returned, (((0,), (0,)), ((), ())), preferred_element_type=jnp.float32
    )
    weighted = expert_out * flat_gate[:, None]
    return jnp.sum(weighted.reshape(tok_count, top_count, width), axis=1).astype(jnp.bfloat16)


def solution(mesh):
    return jax.shard_map(
        body,
        mesh=mesh,
        in_specs=(
            P(("grp", "loc"), None),
            P(("grp", "loc"), None),
            P(("grp", "loc"), None),
            P(("grp", "loc"), None, None),
            P(("grp", "loc"), None, None),
            P(("grp", "loc"), None, None),
            P(),
        ),
        out_specs=P(("grp", "loc"), None),
        check_vma=False,
    )
```

profile of v0, /device:TPU:21, one launch (start us, length us, event | category | flops | bytes accessed | tf_op | source)
XLA Modules:
  0.0 1035.1 jit_solution(8914455513564625300)
XLA Ops:
  0.0 0.0 copy-start
  0.0 0.9 fusion.16
  0.9 0.7 broadcast_compare_fusion
  1.6 0.2 reduce_window_sum.11
  1.8 0.8 select_reduce_fusion
  2.6 0.1 broadcast_and_fusion
  2.8 0.0 copy-done
  2.8 6.1 convolution_convert_fusion
  8.8 13.2 %reshape.85 = bf16[32,20,7168]{2,1,0:T(8,128)(2,1)} reshape(bf16[640,7168]{1,0:T(8,128)(2,1)} %convolution_convert_fusion) | data formatting | bytes 18350080 | tf_op jit(solution)/shard_map/reshape | solution.py:75
  22.1 0.0 copy-start.8
  22.1 6.2 all-to-all-start
  28.3 1.3 collective-permute-start
  29.6 0.2 collective-permute-start.1
  29.8 1.2 collective-permute-start.2
  31.1 0.2 collective-permute-start.3
  31.3 4.1 collective-permute-start.4
  35.4 392.2 %collective-permute-done = bf16[1,7168,256]{2,1,0:T(8,128)(2,1)} collective-permute-done((bf16[1,7168,256]{2,1,0:T(8,128)(2,1)}, bf16[1,7168,256]{2,1,0:T(8,128)(2,1)}, u32[]{:S(2)}, u32[]{:S(2)}) %collective-permute-start) | collective-permute-done | bytes 3670048 | tf_op jit(solution)/shard_map/ppermute | solution.py:12
  427.7 0.0 collective-permute-start.5
  427.7 0.0 copy-done.8
  427.7 0.1 constant_dynamic-slice_fusion
  427.8 0.6 fusion.21
  429.7 76.3 %collective-permute-done.1 = bf16[1,7168,256]{2,1,0:T(8,128)(2,1)} collective-permute-done((bf16[1,7168,256]{2,1,0:T(8,128)(2,1)}, bf16[1,7168,256]{2,1,0:T(8,128)(2,1)}, u32[]{:S(2)}, u32[]{:S(2)}) %collective-permute-start.1) | collective-permute-done | bytes 3670048 | tf_op jit(solution)/shard_map/ppermute | solution.py:12
  506.0 79.0 %collective-permute-done.2 = bf16[1,7168,256]{2,1,0:T(8,128)(2,1)} collective-permute-done((bf16[1,7168,256]{2,1,0:T(8,128)(2,1)}, bf16[1,7168,256]{2,1,0:T(8,128)(2,1)}, u32[]{:S(2)}, u32[]{:S(2)}) %collective-permute-start.2) | collective-permute-done | bytes 3670048 | tf_op jit(solution)/shard_map/ppermute | solution.py:12
  585.0 78.3 %collective-permute-done.3 = bf16[1,7168,256]{2,1,0:T(8,128)(2,1)} collective-permute-done((bf16[1,7168,256]{2,1,0:T(8,128)(2,1)}, bf16[1,7168,256]{2,1,0:T(8,128)(2,1)}, u32[]{:S(2)}, u32[]{:S(2)}) %collective-permute-start.3) | collective-permute-done | bytes 3670048 | tf_op jit(solution)/shard_map/ppermute | solution.py:12
  663.3 9.8 select_bitcast_fusion.1
  673.1 1.6 slice.44
  674.8 1.3 slice.45
  676.1 1.4 slice.43
  677.4 1.3 slice.42
  678.8 63.5 %collective-permute-done.4 = bf16[1,256,7168]{2,1,0:T(8,128)(2,1)} collective-permute-done((bf16[1,256,7168]{2,1,0:T(8,128)(2,1)}, bf16[1,256,7168]{2,1,0:T(8,128)(2,1)}, u32[]{:S(2)}, u32[]{:S(2)}) %collective-permute-start.4) | collective-permute-done | bytes 3670048 | tf_op jit(solution)/shard_map/ppermute | solution.py:12
  742.3 0.0 collective-permute-done.5
  742.3 0.0 copy-done.3
  742.3 4.6 fusion.14
  746.9 0.0 all-to-all-done
  746.9 13.3 %reshape.86 = bf16[640,7168]{1,0:T(8,128)(2,1)} reshape(bf16[32,20,7168]{2,1,0:T(8,128)(2,1)} %all-to-all-done) | data formatting | bytes 18350080 | tf_op jit(solution)/shard_map/reshape | solution.py:77
  760.2 6.8 fusion.6
  767.0 0.0 copy-done.2
  767.0 0.4 copy-done.4
  767.4 0.5 copy-done.5
  768.0 2.5 fusion.2
  770.5 0.0 copy-done.6
  770.5 0.0 copy-done.7
  770.5 5.0 convolution_convert_fusion.1
  775.5 13.2 %reshape.87 = bf16[32,20,7168]{2,1,0:T(8,128)(2,1)} reshape(bf16[640,7168]{1,0:T(8,128)(2,1)} %convolution_convert_fusion.1) | data formatting | bytes 18350080 | tf_op jit(solution)/shard_map/reshape | solution.py:79
  788.7 243.0 %all_to_all.10 = bf16[32,20,7168]{2,1,0:T(8,128)(2,1)S(1)} all-to-all(bf16[32,20,7168]{2,1,0:T(8,128)(2,1)} %reshape.87), channel_id=1, replica_groups=mesh['grp'=8,'loc'=4] {'grp','loc'}, dimensions={0} | all-to-all | bytes 18350080 | tf_op jit(solution)/shard_map/all_to_all | solution.py:78
  1031.8 0.0 copy-done.9
  1031.8 3.4 fusion.1
  1035.1 0.0 copy-done.1
  (12 shorter events, 0.1 us)
Async XLA Ops:
  0.0 2.8 copy-start
  22.1 405.6 %copy-start.8 = (s32[32,2]{0,1:T(2,128)S(1)}, s32[32,2]{0,1:T(2,128)}, u32[]{:S(2)}) copy-start(s32[32,2]{0,1:T(2,128)} %param.13) | copy-start | bytes 772
  22.1 724.8 %all-to-all-start = ((bf16[32,20,7168]{2,1,0:T(8,128)(2,1)}), bf16[32,20,7168]{2,1,0:T(8,128)(2,1)}, u32[]{:S(2)}, u32[]{:S(2)}) async-start(bf16[32,20,7168]{2,1,0:T(8,128)(2,1)} %reshape.85), calls=%async_computation | async-start | bytes 22020096 | tf_op jit(solution)/shard_map/all_to_all | solution.py:76
  28.3 399.4 %collective-permute-start = (bf16[1,7168,256]{2,1,0:T(8,128)(2,1)}, bf16[1,7168,256]{2,1,0:T(8,128)(2,1)}, u32[]{:S(2)}, u32[]{:S(2)}) collective-permute-start(bf16[1,7168,256]{2,1,0:T(8,128)(2,1)} %param.10), channel_id=1, source_target_pairs={{31,0},{0,1},{1,2},{2,3},{3,4},{4,5},{5,6},{6,7},{7,8},{8,9},{9,10... | collective-permute-start | bytes 11010056 | tf_op jit(solution)/shard_map/ppermute | solution.py:12
  29.6 476.4 %collective-permute-start.1 = (bf16[1,7168,256]{2,1,0:T(8,128)(2,1)}, bf16[1,7168,256]{2,1,0:T(8,128)(2,1)}, u32[]{:S(2)}, u32[]{:S(2)}) collective-permute-start(bf16[1,7168,256]{2,1,0:T(8,128)(2,1)} %param.10), channel_id=1, source_target_pairs={{1,0},{2,1},{3,2},{4,3},{5,4},{6,5},{7,6},{8,7},{9,8},{10,9},{11,1... | collective-permute-start | bytes 11010056 | tf_op jit(solution)/shard_map/ppermute | solution.py:12
  29.8 555.1 %collective-permute-start.2 = (bf16[1,7168,256]{2,1,0:T(8,128)(2,1)}, bf16[1,7168,256]{2,1,0:T(8,128)(2,1)}, u32[]{:S(2)}, u32[]{:S(2)}) collective-permute-start(bf16[1,7168,256]{2,1,0:T(8,128)(2,1)} %param.11), channel_id=1, source_target_pairs={{31,0},{0,1},{1,2},{2,3},{3,4},{4,5},{5,6},{6,7},{7,8},{8,9},{9,10... | collective-permute-start | bytes 11010056 | tf_op jit(solution)/shard_map/ppermute | solution.py:12
  31.1 632.2 %collective-permute-start.3 = (bf16[1,7168,256]{2,1,0:T(8,128)(2,1)}, bf16[1,7168,256]{2,1,0:T(8,128)(2,1)}, u32[]{:S(2)}, u32[]{:S(2)}) collective-permute-start(bf16[1,7168,256]{2,1,0:T(8,128)(2,1)} %param.11), channel_id=1, source_target_pairs={{1,0},{2,1},{3,2},{4,3},{5,4},{6,5},{7,6},{8,7},{9,8},{10,9},{11,1... | collective-permute-start | bytes 11010056 | tf_op jit(solution)/shard_map/ppermute | solution.py:12
  31.3 711.0 %collective-permute-start.4 = (bf16[1,256,7168]{2,1,0:T(8,128)(2,1)}, bf16[1,256,7168]{2,1,0:T(8,128)(2,1)}, u32[]{:S(2)}, u32[]{:S(2)}) collective-permute-start(bf16[1,256,7168]{2,1,0:T(8,128)(2,1)} %param.12), channel_id=1, source_target_pairs={{31,0},{0,1},{1,2},{2,3},{3,4},{4,5},{5,6},{6,7},{7,8},{8,9},{9,10... | collective-permute-start | bytes 11010056 | tf_op jit(solution)/shard_map/ppermute | solution.py:12
  427.7 314.6 %collective-permute-start.5 = (bf16[1,256,7168]{2,1,0:T(8,128)(2,1)}, bf16[1,256,7168]{2,1,0:T(8,128)(2,1)}, u32[]{:S(2)}, u32[]{:S(2)}) collective-permute-start(bf16[1,256,7168]{2,1,0:T(8,128)(2,1)} %param.12), channel_id=1, source_target_pairs={{1,0},{2,1},{3,2},{4,3},{5,4},{6,5},{7,6},{8,7},{9,8},{10,9},{11,1... | collective-permute-start | bytes 11010056 | tf_op jit(solution)/shard_map/ppermute | solution.py:12
  676.1 66.2 %copy-start.3 = (bf16[1,256,7168]{2,1,0:T(8,128)(2,1)S(1)}, bf16[1,256,7168]{2,1,0:T(8,128)(2,1)}, u32[]{:S(2)}) copy-start(bf16[1,256,7168]{2,1,0:T(8,128)(2,1)} %param.12) | copy-start | bytes 11010052
  760.2 6.8 copy-start.2
  760.2 7.2 copy-start.4
  760.2 7.8 copy-start.5
  768.0 2.5 copy-start.6
  768.0 2.5 copy-start.7
  788.7 243.0 %copy-start.9 = (f32[128,1]{0,1:T(1,128)S(1)}, f32[128,1]{0,1:T(1,128)}, u32[]{:S(2)}) copy-start(f32[128,1]{0,1:T(1,128)} %param.9) | copy-start | bytes 1540
  1031.8 3.4 copy-start.1
where the time goes:
time: 1040 us
  waiting for transfers between devices  689 us (66%)
  blocking collectives  243 us (23%)
  local copies, waits for them, and re-layouts  47.1 us (5%)
  matrix products  23.7 us (2%)
  other arithmetic  17.1 us (2%)
  starting transfers between devices  13.4 us (1%)
    ppermute x6, waiting for transfers between devices, shifted(): return lax.ppermute(block, axis, route)  689 us
    all_to_all x1, blocking collectives, body(): lax.all_to_all(result.reshape(received.shape), ('grp', 'loc'), split_axis...  243 us
  transfers between devices with their start and end apart: 7, of which 5 were waited for; matrix products, arithmetic and copies ran while one was open for 2% of the time, Pallas kernels for 0%

commit v1 on v0

v1 whole, which is shorter than its diff:
```python
import jax
import jax.numpy as jnp
from jax import lax
from jax.sharding import PartitionSpec as P

SPAN = 4
AXES = ("grp", "loc")


def half_pass(rows, w_gate, w_up, w_down, scale):
    gate_part = jnp.dot(rows, w_gate, preferred_element_type=jnp.float32)
    up_part = jnp.dot(rows, w_up, preferred_element_type=jnp.float32)
    hidden = (jax.nn.silu(gate_part) * up_part * scale[None, :]).astype(jnp.bfloat16)
    return jnp.dot(hidden, w_down, preferred_element_type=jnp.float32)


def body(tokens, route, gate_prob, w_gate, w_up, w_down, partner):
    slots_all = lax.axis_size(AXES)
    own = lax.axis_index(AXES)
    tok_count, top_count = route.shape
    width = tokens.shape[1]
    hid = w_gate.shape[2]
    capacity = max(2, tok_count * top_count * SPAN * 5 // (4 * slots_all))
    experts_all = slots_all // SPAN
    flat_route = route.reshape(-1)
    flat_gate = gate_prob.reshape(-1)
    own_expert = own // SPAN
    place = own % SPAN

    pairs = []
    for i in range(slots_all):
        if i % SPAN == 0:
            pairs.append((i, (i - SPAN) % slots_all))
        elif i % SPAN == SPAN - 1:
            pairs.append((i, (i + SPAN) % slots_all))
    edge_gate, edge_up, edge_down = [
        lax.ppermute(w[0], AXES, pairs) for w in (w_gate, w_up, w_down)
    ]
    mine = lax.dynamic_slice_in_dim(partner, own_expert * SPAN, SPAN, axis=0)
    edge_slot = jnp.where(place == 0, own + SPAN, own - SPAN + slots_all) % slots_all
    is_edge = (place == 0) | (place == SPAN - 1)
    own_times = jnp.sum(mine == own, axis=0).astype(jnp.float32)
    edge_times = jnp.sum((mine == edge_slot) & is_edge, axis=0).astype(jnp.float32)
    own_scale = jnp.repeat(own_times, hid // 2)
    edge_scale = jnp.repeat(edge_times, hid // 2)

    onehot = (flat_route[:, None] == jnp.arange(experts_all, dtype=jnp.int32)[None, :]).astype(
        jnp.int32
    )
    slot_rank = jnp.sum(jnp.cumsum(onehot, axis=0) * onehot, axis=1) - 1
    assigned = jnp.repeat(tokens, top_count, axis=0)
    position = flat_route * capacity + slot_rank
    rows = experts_all * capacity
    picker = (jnp.arange(rows, dtype=jnp.int32)[:, None] == position[None, :]).astype(jnp.bfloat16)
    outgoing = jnp.dot(picker, assigned, preferred_element_type=jnp.float32).astype(jnp.bfloat16)

    groups = [[e * SPAN + q for e in range(experts_all)] for q in range(SPAN)]
    spans = [[e * SPAN + q for q in range(SPAN)] for e in range(experts_all)]

    def across(block):
        if lax.axis_size("loc") == SPAN:
            return lax.all_to_all(block, "grp", split_axis=0, concat_axis=0, tiled=True)
        return lax.all_to_all(
            block, AXES, split_axis=0, concat_axis=0, tiled=True, axis_index_groups=groups
        )

    def within(block):
        if lax.axis_size("loc") == SPAN:
            return lax.all_to_all(block, "loc", split_axis=0, concat_axis=0, tiled=True)
        return lax.all_to_all(
            block, AXES, split_axis=0, concat_axis=0, tiled=True, axis_index_groups=spans
        )

    received = across(outgoing)
    if lax.axis_size("loc") == SPAN:
        gathered = lax.all_gather(received, "loc", axis=0, tiled=True)
    else:
        gathered = lax.all_gather(received, AXES, axis=0, tiled=True, axis_index_groups=spans)
    result = half_pass(gathered, w_gate[0], w_up[0], w_down[0], own_scale)
    result = result + half_pass(gathered, edge_gate, edge_up, edge_down, edge_scale)
    partial = result.astype(jnp.bfloat16)
    parts = within(partial).reshape(SPAN, rows, width)
    total = jnp.sum(parts.astype(jnp.float32), axis=0).astype(jnp.bfloat16)
    returned = across(total)
    expert_out = lax.dot_general(
        picker, returned, (((0,), (0,)), ((), ())), preferred_element_type=jnp.float32
    )
    weighted = expert_out * flat_gate[:, None]
    return jnp.sum(weighted.reshape(tok_count, top_count, width), axis=1).astype(jnp.bfloat16)


def solution(mesh):
    return jax.shard_map(
        body,
        mesh=mesh,
        in_specs=(
            P(AXES, None),
            P(AXES, None),
            P(AXES, None),
            P(AXES, None, None),
            P(AXES, None, None),
            P(AXES, None, None),
            P(),
        ),
        out_specs=P(AXES, None),
        check_vma=False,
    )
```

time: 1040 us -> 547 us (0.53)
  waiting for transfers between devices: 689 us -> 153 us
  blocking collectives: 243 us -> 282 us
  matrix products: 23.7 us -> 58.5 us
  local copies, waits for them, and re-layouts: 47.1 us -> 16.7 us
  between operations: 1.49 us -> 13.5 us
    ppermute x6 -> x3, waiting for transfers between devices: 689 us -> 0.01 us  [body(): lax.ppermute(w[0], AXES, pairs)]
    all_gather x0 -> x1, waiting for transfers between devices: none -> 153 us  [body(): gathered = lax.all_gather(received, 'loc', axis=0, tiled=True)]
    reshape x3 -> x0, local copies, waits for them, and re-layouts: 39.8 us -> none  [the longest x1 13.3 us: body(): received.reshape(-1, width)]
    all_to_all x1 -> x3, blocking collectives: 243 us -> 282 us  [the longest x1 207 us: within(): return lax.all_to_all(block, 'loc', split_axis=0, concat_axis=0, tiled=True)]
    dot_general x3 -> x4, matrix products: 14.3 us -> 52.8 us  [the longest x2 40.9 us: half_pass(): return jnp.dot(hidden, w_down, preferred_element_type=jnp.float32)]
    all_to_all x0 -> x4, local copies, waits for them, and re-layouts: none -> 16.6 us  [across(): return lax.all_to_all(block, 'grp', split_axis=0, concat_axis=0, tiled=True)]
  transfers between devices with their start and end apart: 7 -> 4, of which waited for: 5 -> 1; matrix products, arithmetic and copies ran while one was open for 2% -> 6% of each run, Pallas kernels for 0% -> 0%
where the time goes in v1:
time: 547 us; the launch traced here: 541 us
  blocking collectives  282 us (52%)
  waiting for transfers between devices  153 us (28%)
  matrix products  58.5 us (11%)
  local copies, waits for them, and re-layouts  16.7 us (3%)
  between operations  13.5 us (2%)
  other arithmetic  10 us (2%)
  starting transfers between devices  7.54 us (1%)
    all_to_all x1, blocking collectives, within(): return lax.all_to_all(block, 'loc', split_axis=0, concat_axis=0, tiled=True)  207 us
    all_gather x1, waiting for transfers between devices, body(): gathered = lax.all_gather(received, 'loc', axis=0, tiled=True)  153 us
    all_to_all x2, blocking collectives, across(): return lax.all_to_all(block, 'grp', split_axis=0, concat_axis=0, tiled=True)  74.4 us
    dot_general x2, matrix products, half_pass(): return jnp.dot(hidden, w_down, preferred_element_type=jnp.float32)  40.9 us
    all_to_all x4, local copies, waits for them, and re-layouts, across(): return lax.all_to_all(block, 'grp', split_axis=0, concat_axis=0, tiled=True)  16.6 us
    dot_general x2, matrix products, half_pass(): gate_part = jnp.dot(rows, w_gate, preferred_element_type=jnp.float32)  11.9 us
  transfers between devices with their start and end apart: 4, of which 1 were waited for; matrix products, arithmetic and copies ran while one was open for 6% of the time, Pallas kernels for 0%

profile of v1, /device:TPU:21, one launch (start us, length us, event | category | flops | bytes accessed | tf_op | source)
XLA Modules:
  0.0 541.2 jit_solution(9503285021481576325)
XLA Ops:
  6.5 0.0 copy-start
  6.5 0.0 all-gather.2.cloned.1.call-start
  6.5 0.9 fusion.5
  7.4 0.2 reduce_window_sum.11
  7.6 0.8 select_reduce_fusion
  8.4 0.7 add_add_fusion
  9.1 0.0 copy-done
  9.1 2.1 convolution_convert_fusion
  11.2 4.1 all_to_all.22
  15.4 36.7 %all_to_all.33 = bf16[8,20,7168]{2,1,0:T(8,128)(2,1)} all-to-all(bf16[8,20,7168]{2,1,0:T(8,128)(2,1)} %all_to_all.22), channel_id=1, replica_groups=mesh['grp'=8,'loc'=4] {'grp'}, dimensions={0} | all-to-all | bytes 4587520 | tf_op jit(solution)/shard_map/all_to_all | solution.py:62
  52.1 0.0 copy-start.3
  52.1 4.2 all_to_all.24
  56.3 0.0 all-gather.2.cloned.1.call-update
  56.3 2.6 collective-permute-start
  58.9 2.5 collective-permute-start.2
  61.3 2.5 collective-permute-start.1
  63.8 0.0 copy-done.3
  63.8 0.2 fusion.9
  64.0 0.1 broadcast_bitcast_fusion
  64.1 0.1 broadcast_bitcast_fusion.1
  64.2 153.2 %all-gather.2.cloned.1.call-done = bf16[640,7168]{1,0:T(8,128)(2,1)} async-done(((bf16[160,7168]{1,0:T(8,128)(2,1)}), bf16[640,7168]{1,0:T(8,128)(2,1)}) %all-gather.2.cloned.1.call-update) | async-done | bytes 9175056 | tf_op jit(solution)/shard_map/all_gather | solution.py:76
  217.4 0.0 copy-start.2
  217.4 7.3 %fusion.14 = f32[640,256]{1,0:T(8,128)S(1)} fusion(bf16[640,7168]{1,0:T(8,128)(2,1)} %all-gather.2.cloned.1.call-done, bf16[1,7168,256]{2,1,0:T(8,128)(2,1)} %param.10), kind=kOutput, calls=%fused_computation.26 | convolution fusion | flops 2348810240 | bytes 13500416 | tf_op jit(solution)/shard_map/dot_general | solution.py:11
  224.7 0.0 collective-permute-done
  224.7 0.0 copy-done.2
  224.7 4.6 fusion.18
  229.3 21.7 %fusion.10 = f32[640,7168]{1,0:T(8,128)} fusion(bf16[1,256,7168]{2,1,0:T(8,128)(2,1)} %param.12, bf16[640,7168]{1,0:T(8,128)(2,1)} %all-gather.2.cloned.1.call-done, f32[640,256]{1,0:T(8,128)S(1)} %fusion.14, f32[256]{0:T(256)S(1)} %broadcast_bitcast_fusion.1, bf16[1,7168,256]{2,1,0:T(8,128)(2,1)} %param.11), kind=kOutput, calls=%fused_computation.23 | convolution fusion | flops 4698767360 | bytes 35521536 | tf_op jit(solution)/shard_map/dot_general | solution.py:14
  250.9 0.0 collective-permute-done.2
  250.9 0.0 collective-permute-done.1
  250.9 19.3 %add_convert_fusion = bf16[640,7168]{1,0:T(8,128)(2,1)} fusion(f32[640,7168]{1,0:T(8,128)} %fusion.10, bf16[256,7168]{1,0:T(8,128)(2,1)} %collective-permute-done.2, f32[640,256]{1,0:T(8,128)S(1)} %fusion.18, f32[256]{0:T(256)S(1)} %broadcast_bitcast_fusion, bf16[640,7168]{1,0:T(8,128)(2,1)} %all-gather.2.cloned.1.call-done, ...), kind=kOutput, calls=%fused_computation | convolution fusion | flops 4707942400 | bytes 44696576 | tf_op jit(solution)/shard_map/dot_general | solution.py:14
  270.2 207.3 %all_to_all.34 = bf16[4,160,7168]{2,1,0:T(8,128)(2,1)} all-to-all(bf16[4,160,7168]{2,1,0:T(8,128)(2,1)} %bitcast.35), channel_id=1, replica_groups=mesh['grp'=8,'loc'=4] {'loc'}, dimensions={0} | all-to-all | bytes 18350080 | tf_op jit(solution)/shard_map/all_to_all | solution.py:69
  477.5 7.3 %reduce_sum.46 = bf16[160,7168]{1,0:T(8,128)(2,1)} reduce(bf16[4,160,7168]{2,1,0:T(8,128)(2,1)} %all_to_all.34, bf16[]{:T(256)} %constant.64.clone.1), dimensions={0}, to_apply=%region_4.5 | reduce | flops 3440640 | bytes 11468802 | tf_op jit(solution)/shard_map/reduce_sum | solution.py:83
  484.8 4.1 all_to_all.27
  489.0 0.0 copy-start.1
  489.0 37.6 %all_to_all.35 = bf16[8,20,7168]{2,1,0:T(8,128)(2,1)} all-to-all(bf16[8,20,7168]{2,1,0:T(8,128)(2,1)} %all_to_all.27), channel_id=1, replica_groups=mesh['grp'=8,'loc'=4] {'grp'}, dimensions={0} | all-to-all | bytes 4587520 | tf_op jit(solution)/shard_map/all_to_all | solution.py:62
  526.6 0.0 copy-start.4
  526.6 4.2 all_to_all.29
  530.7 0.0 copy-done.4
  530.7 3.6 fusion
  534.3 0.0 copy-done.1
  (2 shorter events, 0.0 us)
Async XLA Ops:
  6.5 2.6 copy-start
  6.5 210.8 %all-gather.2.cloned.1.call-start = ((), (), s32[]{:S(2)}) async-start(), calls=%async_computation.3 | async-start | bytes 11468800 | tf_op jit(solution)/shard_map/all_gather | solution.py:76
  52.1 11.7 %copy-start.3 = (s32[32,2]{0,1:T(2,128)S(1)}, s32[32,2]{0,1:T(2,128)}, u32[]{:S(2)}) copy-start(s32[32,2]{0,1:T(2,128)} %param.13) | copy-start | bytes 772
  56.3 168.4 %collective-permute-start = (bf16[7168,256]{1,0:T(8,128)(2,1)}, bf16[7168,256]{1,0:T(8,128)(2,1)}, u32[]{:S(2)}, u32[]{:S(2)}) collective-permute-start(bf16[7168,256]{1,0:T(8,128)(2,1)} %bitcast.41), channel_id=1, source_target_pairs={{0,28},{3,7},{4,0},{7,11},{8,4},{11,15},{12,8},{15,19},{16,12},{19... | collective-permute-start | bytes 11010056 | tf_op jit(solution)/shard_map/ppermute | solution.py:37
  58.9 192.1 %collective-permute-start.2 = (bf16[256,7168]{1,0:T(8,128)(2,1)}, bf16[256,7168]{1,0:T(8,128)(2,1)}, u32[]{:S(2)}, u32[]{:S(2)}) collective-permute-start(bf16[256,7168]{1,0:T(8,128)(2,1)} %bitcast.37), channel_id=1, source_target_pairs={{0,28},{3,7},{4,0},{7,11},{8,4},{11,15},{12,8},{15,19},{16,12},{19... | collective-permute-start | bytes 11010056 | tf_op jit(solution)/shard_map/ppermute | solution.py:37
  61.3 189.6 %collective-permute-start.1 = (bf16[7168,256]{1,0:T(8,128)(2,1)}, bf16[7168,256]{1,0:T(8,128)(2,1)}, u32[]{:S(2)}, u32[]{:S(2)}) collective-permute-start(bf16[7168,256]{1,0:T(8,128)(2,1)} %bitcast.36), channel_id=1, source_target_pairs={{0,28},{3,7},{4,0},{7,11},{8,4},{11,15},{12,8},{15,19},{16,12},{19... | collective-permute-start | bytes 11010056 | tf_op jit(solution)/shard_map/ppermute | solution.py:37
  217.4 7.3 %copy-start.2 = (bf16[640,7168]{1,0:T(8,128)(2,1)S(1)}, bf16[640,7168]{1,0:T(8,128)(2,1)}, u32[]{:S(2)}) copy-start(bf16[640,7168]{1,0:T(8,128)(2,1)} %all-gather.2.cloned.1.call-done) | copy-start | bytes 27525124
  489.0 45.4 %copy-start.1 = (bf16[128,7168]{1,0:T(8,128)(2,1)S(1)}, bf16[128,7168]{1,0:T(8,128)(2,1)}, u32[]{:S(2)}) copy-start(bf16[128,7168]{1,0:T(8,128)(2,1)} %param.7) | copy-start | bytes 5505028
  526.6 4.2 copy-start.4
Sparse Core Ops, SparseCore 0:
  56.4 160.8 all-gather.1

commit v2 on v1

v2 whole, which is shorter than its diff:
```python
import functools

import jax
import jax.numpy as jnp
from jax import lax
from jax.experimental import pallas as pl
from jax.experimental.pallas import tpu as pltpu
from jax.sharding import PartitionSpec as P

SPAN = 4
AXES = ("grp", "loc")


MESH = pl.DeviceIdType.MESH


def expert_kernel(
    slots_all,
    n_loc,
    chunks,
    x_ref,
    wg_hbm,
    wu_hbm,
    wd_hbm,
    scale_ref,
    o_ref,
    wg,
    wu,
    wd,
    eg,
    eu,
    ed,
    rows_buf,
    up_buf,
    down_buf,
    hid_buf,
    acc_buf,
    load_sem,
    edge_send,
    edge_recv,
    ag_send,
    ag_recv,
    rs_send,
    rs_recv,
    own_sem,
    out_sem,
):
    last = SPAN - 1
    own = lax.axis_index("grp") * n_loc + lax.axis_index("loc")
    place = lax.rem(own, SPAN)
    span_rows, width = rows_buf.shape[2], rows_buf.shape[3]
    hid = wg.shape[1]
    is_edge = (place == 0) | (place == last)

    def device(index):
        index = lax.rem(index + slots_all, slots_all)
        return (lax.div(index, n_loc), lax.rem(index, n_loc))

    barrier = pltpu.get_barrier_semaphore()

    def greet(index):
        pl.semaphore_signal(barrier, inc=1, device_id=device(index), device_id_type=MESH)

    pl.when(place < last)(lambda: greet(own + 1))
    pl.when(place > 0)(lambda: greet(own - 1))

    @pl.when(is_edge)
    def _():
        greet(own + SPAN)
        greet(own - SPAN)

    pl.semaphore_wait(barrier, jnp.where(is_edge, 3, 2))

    edge_target = device(jnp.where(place == 0, own - SPAN, own + SPAN))
    edge_copies = [
        pltpu.make_async_remote_copy(
            src_ref=src,
            dst_ref=dst,
            send_sem=edge_send.at[k],
            recv_sem=edge_recv.at[k],
            device_id=edge_target,
            device_id_type=MESH,
        )
        for k, (src, dst) in enumerate(((wg_hbm, eg), (wu_hbm, eu), (wd_hbm, ed)))
    ]
    loads = [
        pltpu.make_async_copy(src, dst, load_sem.at[k])
        for k, (src, dst) in enumerate(((wg_hbm, wg), (wu_hbm, wu), (wd_hbm, wd)))
    ]

    def mirrored(way, value):
        return value if way == 0 else last - value

    def gather_copy(way, c, step):
        mine = mirrored(way, place)
        source = mirrored(way, jnp.clip(mine - (step - 1), 0, last))
        return pltpu.make_async_remote_copy(
            src_ref=x_ref.at[c] if step == 1 else rows_buf.at[c, source],
            dst_ref=rows_buf.at[c, source],
            send_sem=ag_send.at[way, c, step - 1],
            recv_sem=ag_recv.at[way, c, step - 1],
            device_id=device(own + 1 if way == 0 else own - 1),
            device_id_type=MESH,
        )

    def gather_sends(way, step):
        mine = mirrored(way, place)
        return (mine < last) & (mine >= step - 1)

    def gather_gets(way, step):
        return mirrored(way, place) >= step

    def gather_start(c, step):
        for way in range(2):
            pl.when(gather_sends(way, step))(lambda way=way: gather_copy(way, c, step).start())

    def gather_wait(c, step):
        for way in range(2):
            pl.when(gather_gets(way, step))(lambda way=way: gather_copy(way, c, step).wait_recv())

    def gather_drain(c):
        for step in range(1, SPAN):
            for way in range(2):
                pl.when(gather_sends(way, step))(
                    lambda way=way, step=step: gather_copy(way, c, step).wait_send()
                )

    side = (up_buf, down_buf)

    def reduce_target(way, step):
        mine = mirrored(way, place)
        return mirrored(way, jnp.clip(SPAN + mine - step, 0, last))

    def reduce_copy(way, c, step, first):
        target = reduce_target(way, step)
        return pltpu.make_async_remote_copy(
            src_ref=rows_buf.at[c, target] if first else side[way].at[c, target],
            dst_ref=side[way].at[c, target],
            send_sem=rs_send.at[way, c, step - 1],
            recv_sem=rs_recv.at[way, c, step - 1],
            device_id=device(own + 1 if way == 0 else own - 1),
            device_id_type=MESH,
        )

    def reduce_sends(way, step):
        mine = mirrored(way, place)
        return (mine <= step - 1) & (mine < last) & (mine > 0)

    def reduce_gets(way, step):
        mine = mirrored(way, place)
        return (mine >= 1) & (mine <= step)

    cols = 512 if width % 512 == 0 else 128

    def reduce_start(c, step):
        for way in range(2):
            pl.when(mirrored(way, place) == 0)(
                lambda way=way: reduce_copy(way, c, step, True).start()
            )

            @pl.when(reduce_sends(way, step))
            def _(way=way):
                target = reduce_target(way, step)

                @pl.loop(0, width // cols)
                def _(k):
                    at = pl.ds(pl.multiple_of(k * cols, cols), cols)
                    side[way][c, target, :, at] = (
                        side[way][c, target, :, at].astype(jnp.float32)
                        + rows_buf[c, target, :, at].astype(jnp.float32)
                    ).astype(jnp.bfloat16)

                reduce_copy(way, c, step, False).start()

    def reduce_wait(c, step):
        for way in range(2):
            pl.when(reduce_gets(way, step))(
                lambda way=way: reduce_copy(way, c, step, False).wait_recv()
            )

    def reduce_drain(c):
        for step in range(1, SPAN):
            for way in range(2):
                mine = mirrored(way, place)
                pl.when((mine <= step - 1) & (mine < last))(
                    lambda way=way, step=step: reduce_copy(way, c, step, False).wait_send()
                )

    def out_copy(c):
        return pltpu.make_async_copy(rows_buf.at[c, place], o_ref.at[c], out_sem.at[c])

    def reduce_finish(c):
        @pl.loop(0, width // cols)
        def _(k):
            at = pl.ds(pl.multiple_of(k * cols, cols), cols)
            acc_buf[...] = rows_buf[c, place, :, at].astype(jnp.float32)
            for way in range(2):

                @pl.when(mirrored(way, place) > 0)
                def _(way=way):
                    acc_buf[...] += side[way][c, place, :, at].astype(jnp.float32)

            rows_buf[c, place, :, at] = acc_buf[...].astype(jnp.bfloat16)

        out_copy(c).start()

    total_rows = SPAN * span_rows
    depth = 512 if width % 512 == 0 else 128

    def make_hidden(c, gate_w, up_w, which):
        def step(k, carry):
            gate_part, up_part = carry
            at = pl.ds(pl.multiple_of(k * depth, depth), depth)
            block = rows_buf[c, :, :, at].reshape(total_rows, depth)
            gate_part += jnp.dot(block, gate_w[at, :], preferred_element_type=jnp.float32)
            up_part += jnp.dot(block, up_w[at, :], preferred_element_type=jnp.float32)
            return gate_part, up_part

        zero = jnp.zeros((total_rows, hid), jnp.float32)
        gate_part, up_part = lax.fori_loop(0, width // depth, step, (zero, zero))
        value = gate_part / (1.0 + jnp.exp(-gate_part)) * up_part
        hid_buf[which] = (value * scale_ref[which : which + 1, :]).astype(jnp.bfloat16)

    def make_partial(c, both):
        @pl.loop(0, width // cols)
        def _(k):
            at = pl.ds(pl.multiple_of(k * cols, cols), cols)
            out = jnp.dot(hid_buf[0], wd[:, at], preferred_element_type=jnp.float32)
            if both:
                out += jnp.dot(hid_buf[1], ed[:, at], preferred_element_type=jnp.float32)
            rows_buf[c, :, :, at] = out.astype(jnp.bfloat16).reshape(SPAN, span_rows, cols)

    def compute(c):
        if c == 0:
            for copy in loads:
                copy.wait()
        make_hidden(c, wg, wu, 0)

        @pl.when(is_edge)
        def _():
            if c == 0:
                for copy in edge_copies:
                    copy.wait_recv()
            make_hidden(c, eg, eu, 1)

        gather_drain(c)
        pl.when(is_edge)(lambda: make_partial(c, True))
        pl.when(jnp.logical_not(is_edge))(lambda: make_partial(c, False))

    own_copies = [
        pltpu.make_async_copy(x_ref.at[c], rows_buf.at[c, place], own_sem.at[c])
        for c in range(chunks)
    ]

    gather_start(0, 1)

    @pl.when(is_edge)
    def _():
        for copy in edge_copies:
            copy.start()

    for copy in own_copies + loads:
        copy.start()
    for step in range(1, SPAN):
        if step > 1:
            gather_start(0, step)
        gather_wait(0, step)
    for c in range(chunks):
        if c == 0:
            for copy in own_copies:
                copy.wait()
        if c + 1 < chunks:
            gather_start(c + 1, 1)
        if c > 0:
            pass
        compute(c)
        reduce_start(c, 1)
        if c + 1 < chunks:
            gather_wait(c + 1, 1)
            gather_start(c + 1, 2)
        reduce_wait(c, 1)
        reduce_start(c, 2)
        if c + 1 < chunks:
            gather_wait(c + 1, 2)
            gather_start(c + 1, 3)
        reduce_wait(c, 2)
        reduce_start(c, 3)
        if c + 1 < chunks:
            gather_wait(c + 1, 3)
        reduce_wait(c, 3)
        reduce_finish(c)
    for c in range(chunks):
        reduce_drain(c)
        out_copy(c).wait()

    @pl.when(is_edge)
    def _():
        for copy in edge_copies:
            copy.wait_send()


def run_experts(received, w_gate, w_up, w_down, scales, slots_all):
    rows, width = received.shape
    hid = w_gate.shape[1]
    chunks = 2 if rows % 32 == 0 else 1
    span_rows = rows // chunks
    anywhere = pl.BlockSpec(memory_space=pl.ANY)
    dma = pltpu.SemaphoreType.DMA
    bf16 = jnp.bfloat16
    out = pl.pallas_call(
        functools.partial(expert_kernel, slots_all, lax.axis_size("loc"), chunks),
        out_shape=jax.ShapeDtypeStruct((chunks, span_rows, width), bf16),
        in_specs=[anywhere] * 4 + [pl.BlockSpec(memory_space=pltpu.VMEM)],
        out_specs=anywhere,
        scratch_shapes=[
            pltpu.VMEM((width, hid), bf16),
            pltpu.VMEM((width, hid), bf16),
            pltpu.VMEM((hid, width), bf16),
            pltpu.VMEM((width, hid), bf16),
            pltpu.VMEM((width, hid), bf16),
            pltpu.VMEM((hid, width), bf16),
            pltpu.VMEM((chunks, SPAN, span_rows, width), bf16),
            pltpu.VMEM((chunks, SPAN, span_rows, width), bf16),
            pltpu.VMEM((chunks, SPAN, span_rows, width), bf16),
            pltpu.VMEM((2, SPAN * span_rows, hid), bf16),
            pltpu.VMEM((span_rows, 512 if width % 512 == 0 else 128), jnp.float32),
            dma((3,)),
            dma((3,)),
            dma((3,)),
            dma((2, chunks, SPAN - 1)),
            dma((2, chunks, SPAN - 1)),
            dma((2, chunks, SPAN - 1)),
            dma((2, chunks, SPAN - 1)),
            dma((chunks,)),
            dma((chunks,)),
        ],
        compiler_params=pltpu.CompilerParams(
            collective_id=0, has_side_effects=True, vmem_limit_bytes=62 * 1024 * 1024
        ),
        name="experts",
    )(received.reshape(chunks, span_rows, width), w_gate, w_up, w_down, scales)
    return out.reshape(rows, width)


def body(tokens, route, gate_prob, w_gate, w_up, w_down, partner):
    slots_all = lax.axis_size(AXES)
    own = lax.axis_index(AXES)
    tok_count, top_count = route.shape
    width = tokens.shape[1]
    hid = w_gate.shape[2]
    capacity = max(2, tok_count * top_count * SPAN * 5 // (4 * slots_all))
    experts_all = slots_all // SPAN
    flat_route = route.reshape(-1)
    flat_gate = gate_prob.reshape(-1)
    own_expert = own // SPAN
    place = own % SPAN

    mine = lax.dynamic_slice_in_dim(partner, own_expert * SPAN, SPAN, axis=0)
    edge_slot = jnp.where(place == 0, own + SPAN, own - SPAN + slots_all) % slots_all
    is_edge = (place == 0) | (place == SPAN - 1)
    own_times = jnp.sum(mine == own, axis=0).astype(jnp.float32)
    edge_times = jnp.sum((mine == edge_slot) & is_edge, axis=0).astype(jnp.float32)
    scales = jnp.repeat(jnp.stack([own_times, edge_times]), hid // 2, axis=1)

    onehot = (flat_route[:, None] == jnp.arange(experts_all, dtype=jnp.int32)[None, :]).astype(
        jnp.int32
    )
    slot_rank = jnp.sum(jnp.cumsum(onehot, axis=0) * onehot, axis=1) - 1
    assigned = jnp.repeat(tokens, top_count, axis=0)
    position = flat_route * capacity + slot_rank
    rows = experts_all * capacity
    picker = (jnp.arange(rows, dtype=jnp.int32)[:, None] == position[None, :]).astype(jnp.bfloat16)
    outgoing = jnp.dot(picker, assigned, preferred_element_type=jnp.float32).astype(jnp.bfloat16)

    groups = [[e * SPAN + q for e in range(experts_all)] for q in range(SPAN)]
    def across(block):
        if lax.axis_size("loc") == SPAN:
            return lax.all_to_all(block, "grp", split_axis=0, concat_axis=0, tiled=True)
        return lax.all_to_all(
            block, AXES, split_axis=0, concat_axis=0, tiled=True, axis_index_groups=groups
        )

    received = across(outgoing)
    total = run_experts(
        received.reshape(rows, width), w_gate[0], w_up[0], w_down[0], scales, slots_all
    )
    returned = across(total)
    expert_out = lax.dot_general(
        picker, returned, (((0,), (0,)), ((), ())), preferred_element_type=jnp.float32
    )
    weighted = expert_out * flat_gate[:, None]
    return jnp.sum(weighted.reshape(tok_count, top_count, width), axis=1).astype(jnp.bfloat16)


def solution(mesh):
    return jax.shard_map(
        body,
        mesh=mesh,
        in_specs=(
            P(AXES, None),
            P(AXES, None),
            P(AXES, None),
            P(AXES, None, None),
            P(AXES, None, None),
            P(AXES, None, None),
            P(),
        ),
        out_specs=P(AXES, None),
        check_vma=False,
    )
```

time: 547 us -> 395 us (0.72)
  Pallas kernels: 0 us -> 287 us
  blocking collectives: 282 us -> 43.3 us
  waiting for transfers between devices: 153 us -> 29 us
  matrix products: 58.5 us -> 5.71 us
  between operations: 13.5 us -> 0.04 us
  other arithmetic: 10 us -> 2.73 us
    pallas_call x0 -> x1, Pallas kernels: none -> 287 us  [run_experts(): pl.pallas_call(functools.partial(expert_kernel, slots_all, lax.axis_size(...]
    all_to_all x1 -> x0, blocking collectives: 207 us -> none  [within(): return lax.all_to_all(block, 'loc', split_axis=0, concat_axis=0, tiled=True)]
    all_gather x1 -> x0, waiting for transfers between devices: 153 us -> none  [body(): gathered = lax.all_gather(received, 'loc', axis=0, tiled=True)]
    dot_general x4 -> x0, matrix products: 52.8 us -> none  [the longest x2 40.9 us: half_pass(): return jnp.dot(hidden, w_down, preferred_element_type=jnp.float32)]
    all_to_all x2 -> x1, blocking collectives: 74.4 us -> 43.3 us  [across(): return lax.all_to_all(block, 'grp', split_axis=0, concat_axis=0, tiled=True)]
    all_to_all x0 -> x1, waiting for transfers between devices: none -> 29 us  [across(): return lax.all_to_all(block, 'grp', split_axis=0, concat_axis=0, tiled=True)]
    ppermute x3 -> x0, starting transfers between devices: 7.54 us -> none  [body(): lax.ppermute(w[0], AXES, pairs)]
    reduce_sum x2 -> x1, other arithmetic: 7.5 us -> 0.19 us  [body(): own_times = jnp.sum(mine == own, axis=0).astype(jnp.float32)]
  transfers between devices with their start and end apart: 4 -> 1, of which waited for: 1 -> 1; matrix products, arithmetic and copies ran while one was open for 6% -> 0% of each run, Pallas kernels for 0% -> 0%
where the time goes in v2:
time: 395 us; the launch traced here: 391 us
  Pallas kernels  287 us (73%)
  blocking collectives  43.3 us (11%)
  waiting for transfers between devices  29 us (7%)
  local copies, waits for them, and re-layouts  17.2 us (4%)
  matrix products  5.71 us (1%)
  starting transfers between devices  5.22 us (1%)
    pallas_call x1, Pallas kernels, run_experts(): pl.pallas_call(functools.partial(expert_kernel, slots_all, lax.axis_size(...  287 us
    all_to_all x1, blocking collectives, across(): return lax.all_to_all(block, 'grp', split_axis=0, concat_axis=0, tiled=True)  43.3 us
    all_to_all x1, waiting for transfers between devices, across(): return lax.all_to_all(block, 'grp', split_axis=0, concat_axis=0, tiled=True)  29 us
    all_to_all x3, local copies, waits for them, and re-layouts, across(): return lax.all_to_all(block, 'grp', split_axis=0, concat_axis=0, tiled=True)  12.4 us
  transfers between devices with their start and end apart: 1, of which 1 were waited for; matrix products, arithmetic and copies ran while one was open for 0% of the time, Pallas kernels for 0%

profile of v2, /device:TPU:21, one launch (start us, length us, event | category | flops | bytes accessed | tf_op | source)
XLA Modules:
  0.0 390.6 jit_solution(2297902163822124672)
XLA Ops:
  0.0 0.0 copy-start
  0.0 0.9 fusion.1
  0.9 0.2 reduce_window_sum.11
  1.1 0.8 select_reduce_fusion
  1.9 0.7 add_add_fusion
  2.5 0.0 copy-done
  2.6 2.1 convolution_convert_fusion
  4.7 4.1 %all_to_all.14 = bf16[8,20,7168]{2,1,0:T(8,128)(2,1)} reshape(bf16[160,7168]{1,0:T(8,128)(2,1)} %convolution_convert_fusion) | data formatting | bytes 4587520 | tf_op jit(solution)/shard_map/all_to_all | solution.py:378
  8.8 0.0 copy-start.1
  8.8 5.2 %all-to-all-start = ((bf16[8,20,7168]{2,1,0:T(8,128)(2,1)}), bf16[8,20,7168]{2,1,0:T(8,128)(2,1)}, u32[]{:S(2)}, u32[]{:S(2)}) async-start(bf16[8,20,7168]{2,1,0:T(8,128)(2,1)} %all_to_all.14), calls=%async_computation | async-start | bytes 5505024 | tf_op jit(solution)/shard_map/all_to_all | solution.py:378
  14.1 0.0 copy-done.1
  14.1 0.2 fusion.4
  14.3 0.1 broadcast_bitcast_fusion
  14.3 0.6 copy.10
  14.9 29.0 %all-to-all-done = bf16[8,20,7168]{2,1,0:T(8,128)(2,1)} async-done(((bf16[8,20,7168]{2,1,0:T(8,128)(2,1)}), bf16[8,20,7168]{2,1,0:T(8,128)(2,1)}, u32[]{:S(2)}, u32[]{:S(2)}) %all-to-all-start) | async-done | bytes 2293792 | tf_op jit(solution)/shard_map/all_to_all | solution.py:378
  43.9 4.1 %reshape.45.x_ref = bf16[2,80,7168]{2,1,0:T(8,128)(2,1)} reshape(bf16[8,20,7168]{2,1,0:T(8,128)(2,1)} %all-to-all-done) | data formatting | bytes 4587520 | tf_op jit(solution)/shard_map/reshape | solution.py:341
  48.0 287.4 %experts.1 = bf16[2,80,7168]{2,1,0:T(8,128)(2,1)} custom-call(bf16[2,80,7168]{2,1,0:T(8,128)(2,1)} %reshape.45.x_ref, bf16[7168,256]{1,0:T(8,128)(2,1)} %bitcast.17, bf16[7168,256]{1,0:T(8,128)(2,1)} %bitcast.18, bf16[256,7168]{1,0:T(8,128)(2,1)} %bitcast.19, f32[2,256]{1,0:T(2,128)} %bitcast.20), custom_call_target="tpu_custom_call" | custom-call | tf_op jit(solution)/shard_map/experts/pallas_call | solution.py:310
  335.5 4.1 %all_to_all.16 = bf16[8,20,7168]{2,1,0:T(8,128)(2,1)} reshape(bf16[2,80,7168]{2,1,0:T(8,128)(2,1)} %experts.1) | data formatting | bytes 4587520 | tf_op jit(solution)/shard_map/all_to_all | solution.py:378
  339.6 43.3 %all_to_all.21 = bf16[8,20,7168]{2,1,0:T(8,128)(2,1)} all-to-all(bf16[8,20,7168]{2,1,0:T(8,128)(2,1)} %all_to_all.16), channel_id=1, replica_groups=mesh['grp'=8,'loc'=4] {'grp'}, dimensions={0} | all-to-all | bytes 4587520 | tf_op jit(solution)/shard_map/all_to_all | solution.py:378
  382.9 0.0 copy-start.2
  382.9 4.2 %all_to_all.18 = bf16[160,7168]{1,0:T(8,128)(2,1)} reshape(bf16[8,20,7168]{2,1,0:T(8,128)(2,1)} %all_to_all.21) | data formatting | bytes 4587520 | tf_op jit(solution)/shard_map/all_to_all | solution.py:378
  387.1 0.0 copy-done.2
  387.1 3.6 fusion
  (2 shorter events, 0.0 us)
Async XLA Ops:
  0.0 2.6 copy-start
  8.8 5.2 %copy-start.1 = (s32[32,2]{0,1:T(2,128)S(1)}, s32[32,2]{0,1:T(2,128)}, u32[]{:S(2)}) copy-start(s32[32,2]{0,1:T(2,128)} %param.13) | copy-start | bytes 772
  8.8 35.0 %all-to-all-start = ((bf16[8,20,7168]{2,1,0:T(8,128)(2,1)}), bf16[8,20,7168]{2,1,0:T(8,128)(2,1)}, u32[]{:S(2)}, u32[]{:S(2)}) async-start(bf16[8,20,7168]{2,1,0:T(8,128)(2,1)} %all_to_all.14), calls=%async_computation | async-start | bytes 5505024 | tf_op jit(solution)/shard_map/all_to_all | solution.py:378
  382.9 4.2 %copy-start.2 = (f32[128,1]{0,1:T(1,128)S(1)}, f32[128,1]{0,1:T(1,128)}, u32[]{:S(2)}) copy-start(f32[128,1]{0,1:T(1,128)} %param.9) | copy-start | bytes 1540

commit v3 on v2

--- a/solution.py
+++ b/solution.py
@@ -239,9 +239,11 @@
         @pl.when(is_edge)
         def _():
             if c == 0:
-                for copy in edge_copies:
+                for copy in edge_copies[:2]:
                     copy.wait_recv()
             make_hidden(c, eg, eu, 1)
+            if c == 0:
+                edge_copies[2].wait_recv()
 
         gather_drain(c)
         pl.when(is_edge)(lambda: make_partial(c, True))
@@ -265,30 +267,29 @@
         if step > 1:
             gather_start(0, step)
         gather_wait(0, step)
+    for copy in own_copies:
+        copy.wait()
+    if chunks > 1:
+        gather_start(1, 1)
+    compute(0)
     for c in range(chunks):
-        if c == 0:
-            for copy in own_copies:
-                copy.wait()
-        if c + 1 < chunks:
-            gather_start(c + 1, 1)
+        more = c + 1 < chunks
+        reduce_start(c, 1)
         if c > 0:
-            pass
-        compute(c)
-        reduce_start(c, 1)
-        if c + 1 < chunks:
-            gather_wait(c + 1, 1)
-            gather_start(c + 1, 2)
-        reduce_wait(c, 1)
-        reduce_start(c, 2)
-        if c + 1 < chunks:
-            gather_wait(c + 1, 2)
-            gather_start(c + 1, 3)
-        reduce_wait(c, 2)
-        reduce_start(c, 3)
-        if c + 1 < chunks:
-            gather_wait(c + 1, 3)
-        reduce_wait(c, 3)
-        reduce_finish(c)
+            reduce_finish(c - 1)
+        for step in range(1, SPAN - 1):
+            if more:
+                gather_wait(c + 1, step)
+                gather_start(c + 1, step + 1)
+            reduce_wait(c, step)
+            reduce_start(c, step + 1)
+        if more:
+            gather_wait(c + 1, SPAN - 1)
+            if c + 2 < chunks:
+                gather_start(c + 2, 1)
+            compute(c + 1)
+        reduce_wait(c, SPAN - 1)
+    reduce_finish(chunks - 1)
     for c in range(chunks):
         reduce_drain(c)
         out_copy(c).wait()

time: 395 us -> 378 us (0.957)
  Pallas kernels: 287 us -> 271 us
    pallas_call x1, Pallas kernels: 287 us -> 271 us  [run_experts(): pl.pallas_call(functools.partial(expert_kernel, slots_all, lax.axis_size(...]
where the time goes in v3:
time: 378 us; the launch traced here: 373 us
  Pallas kernels  271 us (72%)
  blocking collectives  42.6 us (11%)
  waiting for transfers between devices  29 us (8%)
  local copies, waits for them, and re-layouts  17.2 us (5%)
  matrix products  5.71 us (2%)
  starting transfers between devices  5.22 us (1%)
    pallas_call x1, Pallas kernels, run_experts(): pl.pallas_call(functools.partial(expert_kernel, slots_all, lax.axis_size(...  271 us
    all_to_all x1, blocking collectives, across(): return lax.all_to_all(block, 'grp', split_axis=0, concat_axis=0, tiled=True)  42.6 us
    all_to_all x1, waiting for transfers between devices, across(): return lax.all_to_all(block, 'grp', split_axis=0, concat_axis=0, tiled=True)  29 us
    all_to_all x3, local copies, waits for them, and re-layouts, across(): return lax.all_to_all(block, 'grp', split_axis=0, concat_axis=0, tiled=True)  12.4 us
  transfers between devices with their start and end apart: 1, of which 1 were waited for; matrix products, arithmetic and copies ran while one was open for 0% of the time, Pallas kernels for 0%

profile of v3, /device:TPU:21, one launch (start us, length us, event | category | flops | bytes accessed | tf_op | source)
XLA Modules:
  0.0 373.2 jit_solution(6457873544952633143)
XLA Ops:
  0.0 0.0 copy-start
  0.0 0.9 fusion.1
  0.9 0.2 reduce_window_sum.11
  1.1 0.8 select_reduce_fusion
  1.9 0.7 add_add_fusion
  2.5 0.0 copy-done
  2.6 2.1 convolution_convert_fusion
  4.7 4.1 %all_to_all.14 = bf16[8,20,7168]{2,1,0:T(8,128)(2,1)} reshape(bf16[160,7168]{1,0:T(8,128)(2,1)} %convolution_convert_fusion) | data formatting | bytes 4587520 | tf_op jit(solution)/shard_map/all_to_all | solution.py:379
  8.8 0.0 copy-start.1
  8.8 5.2 %all-to-all-start = ((bf16[8,20,7168]{2,1,0:T(8,128)(2,1)}), bf16[8,20,7168]{2,1,0:T(8,128)(2,1)}, u32[]{:S(2)}, u32[]{:S(2)}) async-start(bf16[8,20,7168]{2,1,0:T(8,128)(2,1)} %all_to_all.14), calls=%async_computation | async-start | bytes 5505024 | tf_op jit(solution)/shard_map/all_to_all | solution.py:379
  14.1 0.0 copy-done.1
  14.1 0.2 fusion.4
  14.3 0.1 broadcast_bitcast_fusion
  14.3 0.6 copy.10
  14.9 29.0 %all-to-all-done = bf16[8,20,7168]{2,1,0:T(8,128)(2,1)} async-done(((bf16[8,20,7168]{2,1,0:T(8,128)(2,1)}), bf16[8,20,7168]{2,1,0:T(8,128)(2,1)}, u32[]{:S(2)}, u32[]{:S(2)}) %all-to-all-start) | async-done | bytes 2293792 | tf_op jit(solution)/shard_map/all_to_all | solution.py:379
  43.9 4.1 %reshape.45.x_ref = bf16[2,80,7168]{2,1,0:T(8,128)(2,1)} reshape(bf16[8,20,7168]{2,1,0:T(8,128)(2,1)} %all-to-all-done) | data formatting | bytes 4587520 | tf_op jit(solution)/shard_map/reshape | solution.py:342
  48.0 270.7 %experts.1 = bf16[2,80,7168]{2,1,0:T(8,128)(2,1)} custom-call(bf16[2,80,7168]{2,1,0:T(8,128)(2,1)} %reshape.45.x_ref, bf16[7168,256]{1,0:T(8,128)(2,1)} %bitcast.17, bf16[7168,256]{1,0:T(8,128)(2,1)} %bitcast.18, bf16[256,7168]{1,0:T(8,128)(2,1)} %bitcast.19, f32[2,256]{1,0:T(2,128)} %bitcast.20), custom_call_target="tpu_custom_call" | custom-call | tf_op jit(solution)/shard_map/experts/pallas_call | solution.py:311
  318.7 4.1 %all_to_all.16 = bf16[8,20,7168]{2,1,0:T(8,128)(2,1)} reshape(bf16[2,80,7168]{2,1,0:T(8,128)(2,1)} %experts.1) | data formatting | bytes 4587520 | tf_op jit(solution)/shard_map/all_to_all | solution.py:379
  322.9 42.6 %all_to_all.21 = bf16[8,20,7168]{2,1,0:T(8,128)(2,1)} all-to-all(bf16[8,20,7168]{2,1,0:T(8,128)(2,1)} %all_to_all.16), channel_id=1, replica_groups=mesh['grp'=8,'loc'=4] {'grp'}, dimensions={0} | all-to-all | bytes 4587520 | tf_op jit(solution)/shard_map/all_to_all | solution.py:379
  365.4 0.0 copy-start.2
  365.4 4.2 %all_to_all.18 = bf16[160,7168]{1,0:T(8,128)(2,1)} reshape(bf16[8,20,7168]{2,1,0:T(8,128)(2,1)} %all_to_all.21) | data formatting | bytes 4587520 | tf_op jit(solution)/shard_map/all_to_all | solution.py:379
  369.6 0.0 copy-done.2
  369.6 3.6 fusion
  (2 shorter events, 0.0 us)
Async XLA Ops:
  0.0 2.6 copy-start
  8.8 5.2 %copy-start.1 = (s32[32,2]{0,1:T(2,128)S(1)}, s32[32,2]{0,1:T(2,128)}, u32[]{:S(2)}) copy-start(s32[32,2]{0,1:T(2,128)} %param.13) | copy-start | bytes 772
  8.8 35.0 %all-to-all-start = ((bf16[8,20,7168]{2,1,0:T(8,128)(2,1)}), bf16[8,20,7168]{2,1,0:T(8,128)(2,1)}, u32[]{:S(2)}, u32[]{:S(2)}) async-start(bf16[8,20,7168]{2,1,0:T(8,128)(2,1)} %all_to_all.14), calls=%async_computation | async-start | bytes 5505024 | tf_op jit(solution)/shard_map/all_to_all | solution.py:379
  365.4 4.2 %copy-start.2 = (f32[128,1]{0,1:T(1,128)S(1)}, f32[128,1]{0,1:T(1,128)}, u32[]{:S(2)}) copy-start(f32[128,1]{0,1:T(1,128)} %param.9) | copy-start | bytes 1540

commit v4 on v3

--- a/solution.py
+++ b/solution.py
@@ -42,12 +42,21 @@
     ag_recv,
     rs_send,
     rs_recv,
+    stage_in,
+    stage_out,
+    disp_send,
+    disp_recv,
+    ret_send,
+    ret_recv,
     own_sem,
     out_sem,
 ):
     last = SPAN - 1
     own = lax.axis_index("grp") * n_loc + lax.axis_index("loc")
     place = lax.rem(own, SPAN)
+    own_e = lax.div(own, SPAN)
+    experts, capacity = x_ref.shape[0], x_ref.shape[1]
+    per = experts // chunks
     span_rows, width = rows_buf.shape[2], rows_buf.shape[3]
     hid = wg.shape[1]
     is_edge = (place == 0) | (place == last)
@@ -69,7 +78,30 @@
         greet(own + SPAN)
         greet(own - SPAN)
 
-    pl.semaphore_wait(barrier, jnp.where(is_edge, 3, 2))
+    for away in range(1, experts):
+        greet(own + away * SPAN)
+    pl.semaphore_wait(barrier, jnp.where(is_edge, 3, 2) + experts - 1)
+
+    def dispatch_copy(away):
+        peer = lax.rem(own_e + away, experts)
+        return pltpu.make_async_remote_copy(
+            src_ref=x_ref.at[peer],
+            dst_ref=stage_in.at[own_e],
+            send_sem=disp_send.at[away],
+            recv_sem=disp_recv.at[away],
+            device_id=device(peer * SPAN + place),
+            device_id_type=MESH,
+        )
+
+    def return_copy(peer, sender):
+        return pltpu.make_async_remote_copy(
+            src_ref=stage_out.at[peer],
+            dst_ref=o_ref.at[sender],
+            send_sem=ret_send.at[peer],
+            recv_sem=ret_recv.at[sender],
+            device_id=device(peer * SPAN + place),
+            device_id_type=MESH,
+        )
 
     edge_target = device(jnp.where(place == 0, own - SPAN, own + SPAN))
     edge_copies = [
@@ -95,7 +127,7 @@
         mine = mirrored(way, place)
         source = mirrored(way, jnp.clip(mine - (step - 1), 0, last))
         return pltpu.make_async_remote_copy(
-            src_ref=x_ref.at[c] if step == 1 else rows_buf.at[c, source],
+            src_ref=rows_buf.at[c, source],
             dst_ref=rows_buf.at[c, source],
             send_sem=ag_send.at[way, c, step - 1],
             recv_sem=ag_recv.at[way, c, step - 1],
@@ -186,23 +218,41 @@
                     lambda way=way, step=step: reduce_copy(way, c, step, False).wait_send()
                 )
 
-    def out_copy(c):
-        return pltpu.make_async_copy(rows_buf.at[c, place], o_ref.at[c], out_sem.at[c])
-
-    def reduce_finish(c):
+    kept = pltpu.make_async_copy(stage_out.at[own_e], o_ref.at[own_e], out_sem)
+
+    def unpack():
         @pl.loop(0, width // cols)
         def _(k):
             at = pl.ds(pl.multiple_of(k * cols, cols), cols)
-            acc_buf[...] = rows_buf[c, place, :, at].astype(jnp.float32)
+            for j in range(experts):
+                acc_buf[pl.ds(j * capacity, capacity), :] = stage_in[j, :, at].astype(jnp.float32)
+            for c in range(chunks):
+                rows_buf[c, place, :, at] = acc_buf[
+                    pl.ds(c * span_rows, span_rows), :
+                ].astype(jnp.bfloat16)
+
+    def reduce_finish(c):
+        first = pl.ds(0, span_rows)
+
+        @pl.loop(0, width // cols)
+        def _(k):
+            at = pl.ds(pl.multiple_of(k * cols, cols), cols)
+            acc_buf[first, :] = rows_buf[c, place, :, at].astype(jnp.float32)
             for way in range(2):
 
                 @pl.when(mirrored(way, place) > 0)
                 def _(way=way):
-                    acc_buf[...] += side[way][c, place, :, at].astype(jnp.float32)
-
-            rows_buf[c, place, :, at] = acc_buf[...].astype(jnp.bfloat16)
-
-        out_copy(c).start()
+                    acc_buf[first, :] += side[way][c, place, :, at].astype(jnp.float32)
+
+            for j in range(per):
+                stage_out[c * per + j, :, at] = acc_buf[
+                    pl.ds(j * capacity, capacity), :
+                ].astype(jnp.bfloat16)
+
+        for j in range(per):
+            peer = c * per + j
+            pl.when(own_e != peer)(lambda peer=peer: return_copy(peer, own_e).start())
+            pl.when(own_e == peer)(lambda: kept.start())
 
     total_rows = SPAN * span_rows
     depth = 512 if width % 512 == 0 else 128
@@ -249,26 +299,27 @@
         pl.when(is_edge)(lambda: make_partial(c, True))
         pl.when(jnp.logical_not(is_edge))(lambda: make_partial(c, False))
 
-    own_copies = [
-        pltpu.make_async_copy(x_ref.at[c], rows_buf.at[c, place], own_sem.at[c])
-        for c in range(chunks)
-    ]
-
-    gather_start(0, 1)
+    own_copy = pltpu.make_async_copy(x_ref.at[own_e], stage_in.at[own_e], own_sem)
+    own_copy.start()
+    for away in range(1, experts):
+        dispatch_copy(away).start()
 
     @pl.when(is_edge)
     def _():
         for copy in edge_copies:
             copy.start()
 
-    for copy in own_copies + loads:
+    for copy in loads:
         copy.start()
+    own_copy.wait()
+    for away in range(1, experts):
+        dispatch_copy(away).wait_recv()
+    unpack()
+    gather_start(0, 1)
     for step in range(1, SPAN):
         if step > 1:
             gather_start(0, step)
         gather_wait(0, step)
-    for copy in own_copies:
-        copy.wait()
     if chunks > 1:
         gather_start(1, 1)
     compute(0)
@@ -292,7 +343,16 @@
     reduce_finish(chunks - 1)
     for c in range(chunks):
         reduce_drain(c)
-        out_copy(c).wait()
+    for away in range(1, experts):
+        dispatch_copy(away).wait_send()
+    for peer in range(experts):
+
+        @pl.when(own_e != peer)
+        def _(peer=peer):
+            return_copy(peer, peer).wait_send()
+            return_copy(peer, peer).wait_recv()
+
+    kept.wait()
 
     @pl.when(is_edge)
     def _():
@@ -301,16 +361,17 @@
 
 
 def run_experts(received, w_gate, w_up, w_down, scales, slots_all):
-    rows, width = received.shape
+    experts, capacity, width = received.shape
+    rows = experts * capacity
     hid = w_gate.shape[1]
-    chunks = 2 if rows % 32 == 0 else 1
+    chunks = 2 if rows % 32 == 0 and experts % 2 == 0 else 1
     span_rows = rows // chunks
     anywhere = pl.BlockSpec(memory_space=pl.ANY)
     dma = pltpu.SemaphoreType.DMA
     bf16 = jnp.bfloat16
     out = pl.pallas_call(
         functools.partial(expert_kernel, slots_all, lax.axis_size("loc"), chunks),
-        out_shape=jax.ShapeDtypeStruct((chunks, span_rows, width), bf16),
+        out_shape=jax.ShapeDtypeStruct((experts, capacity, width), bf16),
         in_specs=[anywhere] * 4 + [pl.BlockSpec(memory_space=pltpu.VMEM)],
         out_specs=anywhere,
         scratch_shapes=[
@@ -324,7 +385,7 @@
             pltpu.VMEM((chunks, SPAN, span_rows, width), bf16),
             pltpu.VMEM((chunks, SPAN, span_rows, width), bf16),
             pltpu.VMEM((2, SPAN * span_rows, hid), bf16),
-            pltpu.VMEM((span_rows, 512 if width % 512 == 0 else 128), jnp.float32),
+            pltpu.VMEM((rows, 512 if width % 512 == 0 else 128), jnp.float32),
             dma((3,)),
             dma((3,)),
             dma((3,)),
@@ -332,15 +393,21 @@
             dma((2, chunks, SPAN - 1)),
             dma((2, chunks, SPAN - 1)),
             dma((2, chunks, SPAN - 1)),
-            dma((chunks,)),
-            dma((chunks,)),
+            pltpu.VMEM((experts, capacity, width), bf16),
+            pltpu.VMEM((experts, capacity, width), bf16),
+            dma((experts,)),
+            dma((experts,)),
+            dma((experts,)),
+            dma((experts,)),
+            dma,
+            dma,
         ],
         compiler_params=pltpu.CompilerParams(
             collective_id=0, has_side_effects=True, vmem_limit_bytes=62 * 1024 * 1024
         ),
         name="experts",
-    )(received.reshape(chunks, span_rows, width), w_gate, w_up, w_down, scales)
-    return out.reshape(rows, width)
+    )(received, w_gate, w_up, w_down, scales)
+    return out
 
 
 def body(tokens, route, gate_prob, w_gate, w_up, w_down, partner):
@@ -373,19 +440,14 @@
     picker = (jnp.arange(rows, dtype=jnp.int32)[:, None] == position[None, :]).astype(jnp.bfloat16)
     outgoing = jnp.dot(picker, assigned, preferred_element_type=jnp.float32).astype(jnp.bfloat16)
 
-    groups = [[e * SPAN + q for e in range(experts_all)] for q in range(SPAN)]
-    def across(block):
-        if lax.axis_size("loc") == SPAN:
-            return lax.all_to_all(block, "grp", split_axis=0, concat_axis=0, tiled=True)
-        return lax.all_to_all(
-            block, AXES, split_axis=0, concat_axis=0, tiled=True, axis_index_groups=groups
-        )
-
-    received = across(outgoing)
-    total = run_experts(
-        received.reshape(rows, width), w_gate[0], w_up[0], w_down[0], scales, slots_all
-    )
-    returned = across(total)
+    returned = run_experts(
+        outgoing.reshape(experts_all, capacity, width),
+        w_gate[0],
+        w_up[0],
+        w_down[0],
+        scales,
+        slots_all,
+    ).reshape(rows, width)
     expert_out = lax.dot_general(
         picker, returned, (((0,), (0,)), ((), ())), preferred_element_type=jnp.float32
     )

time: 378 us -> 337 us (0.89); the launches traced: 373 us -> 337 us
  Pallas kernels: 271 us -> 319 us
  blocking collectives: 42.6 us -> 0 us
  waiting for transfers between devices: 29 us -> 0 us
  local copies, waits for them, and re-layouts: 17.2 us -> 8.94 us
  starting transfers between devices: 5.22 us -> 0 us
    pallas_call x1, Pallas kernels: 271 us -> 319 us  [run_experts(): pl.pallas_call(functools.partial(expert_kernel, slots_all, lax.axis_size(...]
    all_to_all x1 -> x0, blocking collectives: 42.6 us -> none  [across(): return lax.all_to_all(block, 'grp', split_axis=0, concat_axis=0, tiled=True)]
    all_to_all x1 -> x0, waiting for transfers between devices: 29 us -> none  [across(): return lax.all_to_all(block, 'grp', split_axis=0, concat_axis=0, tiled=True)]
    all_to_all x3 -> x0, local copies, waits for them, and re-layouts: 12.4 us -> none  [across(): return lax.all_to_all(block, 'grp', split_axis=0, concat_axis=0, tiled=True)]
    all_to_all x1 -> x0, starting transfers between devices: 5.22 us -> none  [across(): return lax.all_to_all(block, 'grp', split_axis=0, concat_axis=0, tiled=True)]
    reshape x1 -> x2, local copies, waits for them, and re-layouts: 4.15 us -> 8.28 us  [the longest x1 4.14 us: body(): returned = run_experts(outgoing.reshape(experts_all, capacity, width), w_...]
  transfers between devices with their start and end apart: 1 -> 0, of which waited for: 1 -> 0; matrix products, arithmetic and copies ran while one was open for 0% -> 0% of each run, Pallas kernels for 0% -> 0%
where the time goes in v4:
time: 337 us
  Pallas kernels  319 us (95%)
  local copies, waits for them, and re-layouts  8.94 us (3%)
  matrix products  5.72 us (2%)
  other arithmetic  3.44 us (1%)
    pallas_call x1, Pallas kernels, run_experts(): pl.pallas_call(functools.partial(expert_kernel, slots_all, lax.axis_size(...  319 us

profile of v4, /device:TPU:21, one launch (start us, length us, event | category | flops | bytes accessed | tf_op | source)
XLA Modules:
  0.0 337.1 jit_solution(7707102345011581686)
XLA Ops:
  0.0 0.0 copy-start
  0.0 1.0 fusion.4
  1.1 0.1 broadcast_bitcast_fusion
  1.1 0.6 copy.10
  1.7 0.7 fusion.1
  2.5 0.2 reduce_window_sum.11
  2.6 0.8 select_reduce_fusion
  3.5 0.7 add_add_fusion
  4.1 0.0 copy-done
  4.1 2.2 convolution_convert_fusion
  6.3 4.1 %reshape.41.x_ref = bf16[8,20,7168]{2,1,0:T(8,128)(2,1)} reshape(bf16[160,7168]{1,0:T(8,128)(2,1)} %convolution_convert_fusion) | data formatting | bytes 4587520 | tf_op jit(solution)/shard_map/reshape | solution.py:444
  10.4 318.9 %experts.1 = bf16[8,20,7168]{2,1,0:T(8,128)(2,1)} custom-call(bf16[8,20,7168]{2,1,0:T(8,128)(2,1)} %reshape.41.x_ref, bf16[7168,256]{1,0:T(8,128)(2,1)} %bitcast.17, bf16[7168,256]{1,0:T(8,128)(2,1)} %bitcast.18, bf16[256,7168]{1,0:T(8,128)(2,1)} %bitcast.19, f32[2,256]{1,0:T(2,128)} %bitcast.20), custom_call_target="tpu_custom_call" | custom-call | tf_op jit(solution)/shard_map/experts/pallas_call | solution.py:372
  329.4 0.0 copy-start.1
  329.4 4.1 %reshape.43 = bf16[160,7168]{1,0:T(8,128)(2,1)} reshape(bf16[8,20,7168]{2,1,0:T(8,128)(2,1)} %experts.1) | data formatting | bytes 4587520 | tf_op jit(solution)/shard_map/reshape | solution.py:450
  333.5 0.0 copy-done.1
  333.5 3.6 %fusion = bf16[128,7168]{1,0:T(8,128)(2,1)} fusion(bf16[160,7168]{1,0:T(8,128)(2,1)} %reshape.43, f32[128]{0:T(128)S(1)} %bitcast.23, s32[128]{0:T(128)S(1)} %add_add_fusion), kind=kOutput, calls=%fused_computation.2 | convolution fusion | flops 295456768 | bytes 4129792 | tf_op jit(solution)/shard_map/dot_general | solution.py:451
  (2 shorter events, 0.0 us)
Async XLA Ops:
  0.0 4.1 %copy-start = (bf16[128,7168]{1,0:T(8,128)(2,1)S(1)}, bf16[128,7168]{1,0:T(8,128)(2,1)}, u32[]{:S(2)}) copy-start(bf16[128,7168]{1,0:T(8,128)(2,1)} %param.7) | copy-start | bytes 5505028
  329.4 4.2 %copy-start.1 = (f32[128,1]{0,1:T(1,128)S(1)}, f32[128,1]{0,1:T(1,128)}, u32[]{:S(2)}) copy-start(f32[128,1]{0,1:T(1,128)} %param.9) | copy-start | bytes 1540

commit v5 on v4

--- a/solution.py
+++ b/solution.py
@@ -437,19 +437,22 @@
     assigned = jnp.repeat(tokens, top_count, axis=0)
     position = flat_route * capacity + slot_rank
     rows = experts_all * capacity
-    picker = (jnp.arange(rows, dtype=jnp.int32)[:, None] == position[None, :]).astype(jnp.bfloat16)
-    outgoing = jnp.dot(picker, assigned, preferred_element_type=jnp.float32).astype(jnp.bfloat16)
-
+    places = jnp.arange(rows, dtype=jnp.int32).reshape(experts_all, capacity)
+    picker = (places[:, :, None] == position[None, None, :]).astype(jnp.bfloat16)
+    spread = jnp.broadcast_to(assigned[None], (experts_all,) + assigned.shape)
+    outgoing = lax.dot_general(
+        picker, spread, (((2,), (1,)), ((0,), (0,))), preferred_element_type=jnp.float32
+    ).astype(jnp.bfloat16)
     returned = run_experts(
-        outgoing.reshape(experts_all, capacity, width),
+        outgoing,
         w_gate[0],
         w_up[0],
         w_down[0],
         scales,
         slots_all,
-    ).reshape(rows, width)
+    )
     expert_out = lax.dot_general(
-        picker, returned, (((0,), (0,)), ((), ())), preferred_element_type=jnp.float32
+        picker, returned, (((0, 1), (0, 1)), ((), ())), preferred_element_type=jnp.float32
     )
     weighted = expert_out * flat_gate[:, None]
     return jnp.sum(weighted.reshape(tok_count, top_count, width), axis=1).astype(jnp.bfloat16)

time: 337 us -> 330 us (0.979)
  local copies, waits for them, and re-layouts: 8.94 us -> 0.67 us
    reshape x2 -> x0, local copies, waits for them, and re-layouts: 8.28 us -> none  [the longest x1 4.14 us: body(): returned = run_experts(outgoing.reshape(experts_all, capacity, width), w_...]
where the time goes in v5:
time: 330 us
  Pallas kernels  319 us (97%)
  matrix products  7.14 us (2%)
  other arithmetic  3.45 us (1%)
    pallas_call x1, Pallas kernels, run_experts(): pl.pallas_call(functools.partial(expert_kernel, slots_all, lax.axis_size(...  319 us

profile of v5, /device:TPU:21, one launch (start us, length us, event | category | flops | bytes accessed | tf_op | source)
XLA Modules:
  0.0 330.3 jit_solution(13419678098163364993)
XLA Ops:
  0.0 0.0 copy-start
  0.0 1.0 fusion.10
  1.1 0.1 broadcast_bitcast_fusion
  1.1 0.6 copy.10
  1.7 0.7 fusion.5
  2.5 0.2 reduce_window_sum.11
  2.6 0.8 select_reduce_fusion
  3.5 0.7 add_add_fusion
  4.1 0.0 copy-done
  4.1 3.4 %convolution_convert_fusion.x_ref = bf16[8,20,7168]{2,1,0:T(8,128)(2,1)} fusion(bf16[128,7168]{1,0:T(8,128)(2,1)S(1)} %copy-done, s32[128]{0:T(128)S(1)} %add_add_fusion, s32[8,20]{1,0:T(8,128)S(1)} %multiply_add_fusion), kind=kOutput, calls=%fused_computation | convolution fusion | flops 294768640 | bytes 4129920 | tf_op jit(solution)/shard_map/dot_general | solution.py:443
  7.5 0.0 copy-start.1
  7.5 319.0 %experts.1 = bf16[8,20,7168]{2,1,0:T(8,128)(2,1)} custom-call(bf16[8,20,7168]{2,1,0:T(8,128)(2,1)} %convolution_convert_fusion.x_ref, bf16[7168,256]{1,0:T(8,128)(2,1)} %bitcast.22, bf16[7168,256]{1,0:T(8,128)(2,1)} %bitcast.23, bf16[256,7168]{1,0:T(8,128)(2,1)} %bitcast.24, f32[2,256]{1,0:T(2,128)} %bitcast.25), custom_call_target="tpu_custom_call" | custom-call | tf_op jit(solution)/shard_map/experts/pallas_call | solution.py:372
  326.5 0.0 copy-done.1
  326.5 3.8 %fusion.1 = bf16[128,7168]{1,0:T(8,128)(2,1)} fusion(bf16[8,20,7168]{2,1,0:T(8,128)(2,1)} %experts.1, f32[128]{0:T(128)S(1)} %bitcast.28, s32[128]{0:T(128)S(1)} %add_add_fusion, s32[8,20]{1,0:T(8,128)S(1)} %multiply_add_fusion), kind=kOutput, calls=%fused_computation.3 | convolution fusion | flops 295456768 | bytes 4130432 | tf_op jit(solution)/shard_map/dot_general | solution.py:454
  (3 shorter events, 0.0 us)
Async XLA Ops:
  0.0 4.1 %copy-start = (bf16[128,7168]{1,0:T(8,128)(2,1)S(1)}, bf16[128,7168]{1,0:T(8,128)(2,1)}, u32[]{:S(2)}) copy-start(bf16[128,7168]{1,0:T(8,128)(2,1)} %param.7) | copy-start | bytes 5505028
  7.5 319.0 %copy-start.1 = (f32[128,1]{0,1:T(1,128)S(1)}, f32[128,1]{0,1:T(1,128)}, u32[]{:S(2)}) copy-start(f32[128,1]{0,1:T(1,128)} %param.9) | copy-start | bytes 1540
